TPU v7x, 32 devices: a whole 2x2x4 slice. The times are simulated.
32 devices in a mesh: groups: 2 (over x), ctx: 16 (over z, y, core).
Axes of the slice: x: 2, y: 2, z: 4, core: 2. Of those that a mesh axis runs over, the one named last changes fastest.
Arguments:
- queries: bfloat16 [16384, 1024], P(('groups', 'ctx')), parts along dimension 0, may hold values from -24 to 24
- key_rows: bfloat16 [16384, 1024], P(('groups', 'ctx')), parts along dimension 0, may hold values from -12 to 12
- value_rows: bfloat16 [16384, 1024], P(('groups', 'ctx')), parts along dimension 0, may hold values from -6 to 6
- step_rates: float32 [2, 16384], P(None, ('groups', 'ctx')), parts along dimension 1, may hold values from 0.002 to 0.02
- w_gate: bfloat16 [2048, 512], P('groups'), parts along dimension 0, may hold values from -2 to 2
- w_up: bfloat16 [2048, 512], P('groups'), parts along dimension 0, may hold values from -2 to 2
- w_down: bfloat16 [2048, 512], P('groups'), parts along dimension 0, may hold values from -2 to 2
Outputs:
- layer_out: bfloat16 [16384, 1024], P(('groups', 'ctx')), parts along dimension 0
- new_weights: bfloat16 [6144, 512], P(('groups', 'ctx')), parts along dimension 0
There are 2 independent parts, one for each index of `groups`. A program takes and returns all parts, laid end to end along the dimension named above; each array names one. Nothing has to cross between parts.
All inputs are finite; a program needn't handle non-finite values.
Results may differ from a plain program's by a relative error of at most 0.012.
The roundings to bfloat16 on the way count: a program that leaves them out, or rounds other values in their place, can miss the bound.
Values may be sent and summed in bfloat16 or wider, within the bound.
No kernel may reach another device: no remote copies, remote signals or barrier semaphores. Data moves between devices by JAX's collectives and lax.ppermute only.
A program may use at most 64 MiB of HBM per device.

v0:
```python
import math
import jax
import jax.numpy as jnp
from jax import lax
from jax.sharding import PartitionSpec as P

H = 2
HD = 512
WINDOW = 1024


def passed_along(value, axis, steps):
    count = lax.axis_size(axis)
    leading, last = (max(0, -steps), min(count, count - steps))
    return lax.ppermute(value, axis, [(source, source + steps) for source in range(leading, last)])


def rms_rows(row_values):
    values = row_values.astype(jnp.float32).reshape(row_values.shape[0], H, HD)
    return (values * lax.rsqrt(jnp.mean(values * values, -1, keepdims=True) + 1e-06)).astype(
        jnp.bfloat16
    )


def normalize_rows(old_rows, grad_rows):
    old_values = old_rows.astype(jnp.float32)
    raised = old_values - grad_rows
    factor = jnp.sqrt(jnp.mean(old_values * old_values, -1, keepdims=True) + 1e-06) * lax.rsqrt(
        jnp.mean(raised * raised, -1, keepdims=True) + 1e-06
    )
    return (raised * factor).astype(jnp.bfloat16)


def local(queries, key_rows, value_rows, step_rates, w_gate, w_up, w_down):
    tok_rows = queries.shape[0]
    reach = WINDOW // tok_rows
    earlier_keys = []
    earlier_values = []
    for step in range(reach, 0, -1):
        moved = passed_along((key_rows, value_rows), "ctx", step)
        earlier_keys.append(moved[0])
        earlier_values.append(moved[1])
    all_keys = jnp.concatenate(earlier_keys + [key_rows], 0)
    all_values = jnp.concatenate(earlier_values + [value_rows], 0)
    own_start = lax.axis_index("ctx") * tok_rows
    block_rows = min(512, tok_rows)
    q_block = queries.reshape(block_rows, H, HD)
    k_block = all_keys.reshape(WINDOW + block_rows, H, HD)
    v_block = all_values.reshape(WINDOW + block_rows, H, HD)
    scores = jnp.einsum("qhd,khd->hqk", q_block, k_block, preferred_element_type=jnp.float32) * (
        1.0 / math.sqrt(HD)
    )
    q_pos = 0 + jnp.arange(block_rows, dtype=jnp.int32)
    k_pos = 0 - WINDOW + jnp.arange(WINDOW + block_rows, dtype=jnp.int32)
    allowed = (
        (k_pos[None, :] <= q_pos[:, None])
        & (k_pos[None, :] > q_pos[:, None] - WINDOW)
        & (k_pos[None, :] + own_start >= 0)
    )
    scores = jnp.where(allowed[None], scores, -jnp.inf)
    highest = jnp.max(scores, -1, keepdims=True)
    expo = jnp.exp(scores - highest)
    weights = (expo / jnp.sum(expo, -1, keepdims=True)).astype(jnp.bfloat16)
    result = jnp.einsum("hqk,khd->qhd", weights, v_block, preferred_element_type=jnp.float32)
    pieces = result.astype(jnp.bfloat16)
    q_norm = rms_rows(queries)
    k_norm = rms_rows(key_rows)
    gate_m = w_gate.reshape(H, HD, HD)
    up_m = w_up.reshape(H, HD, HD)
    down_m = w_down.reshape(H, HD, HD)
    pre_gate = jnp.einsum("thd,hjd->thj", k_norm, gate_m, preferred_element_type=jnp.float32)
    pre_up = jnp.einsum("thd,hjd->thj", k_norm, up_m, preferred_element_type=jnp.float32)
    sig = jax.nn.sigmoid(pre_gate)
    active = pre_gate * sig
    gated = (active * pre_up).astype(jnp.bfloat16)
    errors = (-step_rates.T[:, :, None] * pieces.astype(jnp.float32)).astype(jnp.bfloat16)
    grad_down = jnp.einsum("tho,thj->hoj", errors, gated, preferred_element_type=jnp.float32)
    back = jnp.einsum("tho,hoj->thj", errors, down_m, preferred_element_type=jnp.float32)
    d_gate = (back * pre_up * sig * (1.0 + pre_gate * (1.0 - sig))).astype(jnp.bfloat16)
    d_up = (back * active).astype(jnp.bfloat16)
    grad_gate = jnp.einsum("thj,thd->hjd", d_gate, k_norm, preferred_element_type=jnp.float32)
    grad_up = jnp.einsum("thj,thd->hjd", d_up, k_norm, preferred_element_type=jnp.float32)
    grads = jnp.concatenate(
        [grad_gate.reshape(H * HD, HD), grad_up.reshape(H * HD, HD), grad_down.reshape(H * HD, HD)],
        0,
    )
    old_rows = jnp.concatenate([w_gate, w_up, w_down], 0)
    own_count = grads.shape[0] // lax.axis_size("ctx")
    own_first = lax.axis_index("ctx") * own_count
    summed = lax.psum(grads, "ctx")
    fresh = normalize_rows(old_rows, summed)
    own_weights = lax.dynamic_slice_in_dim(fresh, own_first, own_count, 0)
    new_gate = fresh[: H * HD].reshape(H, HD, HD)
    new_up = fresh[H * HD : 2 * H * HD].reshape(H, HD, HD)
    new_down = fresh[2 * H * HD :].reshape(H, HD, HD)
    q_gate = jnp.einsum("thd,hjd->thj", q_norm, new_gate, preferred_element_type=jnp.float32)
    q_up = jnp.einsum("thd,hjd->thj", q_norm, new_up, preferred_element_type=jnp.float32)
    q_gated = (q_gate * jax.nn.sigmoid(q_gate) * q_up).astype(jnp.bfloat16)
    fast_out = jnp.einsum("thj,hoj->tho", q_gated, new_down, preferred_element_type=jnp.float32)
    layer_out = (
        (pieces.astype(jnp.float32) + fast_out).astype(jnp.bfloat16).reshape(tok_rows, H * HD)
    )
    return (layer_out, own_weights)


def solution(mesh):
    return jax.shard_map(
        local,
        mesh=mesh,
        in_specs=(
            P(("groups", "ctx"), None),
            P(("groups", "ctx"), None),
            P(("groups", "ctx"), None),
            P(None, ("groups", "ctx")),
            P("groups", None),
            P("groups", None),
            P("groups", None),
        ),
        out_specs=(P(("groups", "ctx"), None), P(("groups", "ctx"), None)),
        check_vma=False,
    )
```

profile of v0, /device:TPU:0, one launch (start us, length us, event | category | flops | bytes accessed | tf_op | source)
XLA Modules:
  0.0 283.9 jit_solution(13785161849252597991)
XLA Ops:
  7.2 0.0 all-reduce.2.cloned.1.call-start
  7.2 1.5 copy.89
  8.7 5.9 %collective-permute-start.2 = (bf16[512,1024]{0,1:T(8,128)(2,1)S(1)}, bf16[512,1024]{0,1:T(8,128)(2,1)}, u32[]{:S(2)}, u32[]{:S(2)}) collective-permute-start(bf16[512,1024]{0,1:T(8,128)(2,1)S(1)} %copy.89), channel_id=1, source_target_pairs={{0,2},{1,3},{2,4},{3,5},{4,6},{5,7},{6,8},{7,9},{8,10},{9,11},{10,... | collective-permute-start | bytes 3145736 | tf_op jit(solution)/shard_map/ppermute | solution.py:15
  14.6 2.4 collective-permute-start.3
  17.0 3.0 %collective-permute-start = (bf16[512,1024]{1,0:T(8,128)(2,1)}, bf16[512,1024]{1,0:T(8,128)(2,1)}, u32[]{:S(2)}, u32[]{:S(2)}) collective-permute-start(bf16[512,1024]{1,0:T(8,128)(2,1)} %param.9), channel_id=1, source_target_pairs={{0,2},{1,3},{2,4},{3,5},{4,6},{5,7},{6,8},{7,9},{8,10},{9,11},{10,... | collective-permute-start | bytes 3145736 | tf_op jit(solution)/shard_map/ppermute | solution.py:15
  20.0 4.2 %collective-permute-start.1 = (bf16[512,1024]{1,0:T(8,128)(2,1)}, bf16[512,1024]{1,0:T(8,128)(2,1)}, u32[]{:S(2)}, u32[]{:S(2)}) collective-permute-start(bf16[512,1024]{1,0:T(8,128)(2,1)} %param.9), channel_id=1, source_target_pairs={{0,1},{1,2},{2,3},{3,4},{4,5},{5,6},{6,7},{7,8},{8,9},{9,10},{10,1... | collective-permute-start | bytes 3145736 | tf_op jit(solution)/shard_map/ppermute | solution.py:15
  24.2 0.2 multiply_reduce_fusion.1
  24.5 0.0 copy-start.8
  24.5 1.6 copy.99
  26.1 0.0 copy-start.5
  26.1 1.9 multiply_convert_fusion.1
  28.0 0.0 copy-done.8
  28.0 2.2 fusion.59
  30.2 0.0 copy-start.16
  30.2 0.0 copy-start.14
  30.2 0.0 copy-done.5
  30.2 2.1 fusion.58
  32.3 0.0 copy-done.16
  32.3 2.0 fusion.7
  34.3 25.5 %collective-permute-done = bf16[512,1024]{1,0:T(8,128)(2,1)} collective-permute-done((bf16[512,1024]{1,0:T(8,128)(2,1)}, bf16[512,1024]{1,0:T(8,128)(2,1)}, u32[]{:S(2)}, u32[]{:S(2)}) %collective-permute-start) | collective-permute-done | bytes 1048608 | tf_op jit(solution)/shard_map/ppermute | solution.py:15
  59.7 0.0 collective-permute-done.1
  59.7 0.0 copy-done.14
  59.7 3.0 %pad_maximum_fusion.1 = bf16[1536,1024]{1,0:T(8,128)(2,1)} fusion(bf16[512,1024]{1,0:T(8,128)(2,1)S(1)} %copy-done.14, bf16[512,1024]{1,0:T(8,128)(2,1)} %collective-permute-done.1, bf16[512,1024]{1,0:T(8,128)(2,1)} %collective-permute-done), kind=kLoop, calls=%fused_computation.11 | loop fusion | flops 9437184 | bytes 6291456 | tf_op jit(solution)/shard_map/concatenate | solution.py:44
  62.8 4.7 %copy.88 = bf16[1536,1024]{0,1:T(8,128)(2,1)} copy(bf16[1536,1024]{1,0:T(8,128)(2,1)} %pad_maximum_fusion.1) | data formatting | bytes 6291456 | tf_op jit(solution)/shard_map/concatenate | solution.py:44
  67.5 0.0 copy-start.1
  67.5 0.0 collective-permute-done.2
  67.5 0.0 collective-permute-done.3
  67.5 1.9 pad_maximum_fusion.2
  69.4 0.0 copy-done.1
  69.4 0.0 copy-start.15
  69.4 2.4 fusion.31
  71.9 0.0 copy-done.15
  71.9 0.0 copy-start.10
  71.9 2.2 fusion.57
  74.1 0.4 copy-done.10
  74.5 7.7 %fusion.26 = bf16[2,512,512]{2,1,0:T(8,128)(2,1)} fusion(bf16[1536,2,512]{0,2,1:T(8,128)(2,1)} %bitcast.136, f32[2,512]{1,0:T(2,128)S(1)} %fusion.57, f32[2,1536,512]{2,1,0:T(8,128)} %copy-done.10, pred[512,1536]{0,1:T(8,128)(4,1)} %fusion.7), kind=kOutput, calls=%fused_computation.53 | convolution fusion | flops 1619003904 | bytes 11276288 | tf_op jit(solution)/shard_map/hqk,khd->qhd/dot_general | solution.py:64
  82.3 0.0 copy-done.3
  82.3 2.1 fusion.36
  84.4 0.0 copy-done.11
  84.4 0.0 copy-start.12
  84.4 0.9 fusion.27
  85.3 0.7 copy-done.12
  86.0 1.1 fusion.33
  87.1 0.1 copy-done.13
  87.2 1.0 fusion.29
  88.2 3.4 %pad_maximum_fusion = f32[3072,512]{1,0:T(8,128)} fusion(f32[1024,512]{1,0:T(8,128)S(1)} %bitcast.139, f32[1024,512]{1,0:T(8,128)S(1)} %bitcast.137, f32[1024,512]{1,0:T(8,128)S(1)} %bitcast.138), kind=kLoop, calls=%fused_computation.4 | loop fusion | flops 3145728 | bytes 12582912 | tf_op jit(solution)/shard_map/concatenate | solution.py:83
  91.6 0.0 all-reduce.2.cloned.1.call-update
  91.6 0.3 fusion.9
  91.9 162.4 %all-reduce.2.cloned.1.call-done = f32[3072,512]{1,0:T(8,128)} async-done(((f32[3072,512]{1,0:T(8,128)}), f32[3072,512]{1,0:T(8,128)}) %all-reduce.2.cloned.1.call-update) | async-done | bytes 6291472 | tf_op jit(solution)/shard_map/psum | solution.py:90
  254.3 0.0 copy-done.6
  254.3 0.0 copy-start.9
  254.3 4.4 %fusion.1 = (f32[3072]{0:T(1024)S(1)}, f32[3072]{0:T(1024)S(1)}) fusion(bf16[1024,512]{1,0:T(8,128)(2,1)S(1)} %copy-done.3, bf16[1024,512]{1,0:T(8,128)(2,1)S(1)} %copy-done.6, bf16[1024,512]{1,0:T(8,128)(2,1)} %param.11, f32[3072,512]{1,0:T(8,128)} %all-reduce.2.cloned.1.call-done), kind=kLoop, calls=%fused_computation.3 | loop fusion | flops 17295360 | bytes 9461760 | tf_op jit(solution)/shard_map/reduce_sum | solution.py:28
  258.8 0.5 copy-done
  259.2 0.3 copy-done.4
  259.5 0.3 copy-done.7
  259.8 0.3 copy-done.9
  260.1 5.1 %multiply_convert_fusion = bf16[3072,512]{1,0:T(8,128)(2,1)S(1)} fusion(f32[3072,512]{1,0:T(8,128)S(1)} %copy-done, f32[3072]{0:T(1024)S(1)} %rsqrt_multiply_fusion, bf16[1024,512]{1,0:T(8,128)(2,1)S(1)} %copy-done.4, bf16[1024,512]{1,0:T(8,128)(2,1)S(1)} %copy-done.7, bf16[1024,512]{1,0:T(8,128)(2,1)S(1)} %copy-done.9), kind=kLoop, calls=%fused_computation.6 | loop fusion | flops 14155776 | bytes 12595200 | tf_op jit(solution)/shard_map/convert_element_type | solution.py:31
  265.1 0.0 copy-start.2
  265.2 1.5 fusion.56
  266.7 0.0 copy-done.2
  266.7 2.1 fusion.40
  268.8 5.3 %fusion.11 = bf16[512,2,512]{0,2,1:T(8,128)(2,1)} fusion(bf16[2,512,512]{2,1,0:T(8,128)(2,1)} %fusion.26, bf16[2,512,512]{2,1,0:T(8,128)(2,1)} %bitcast.142, f32[2,512,512]{1,2,0:T(8,128)} %fusion.40, bf16[2,512,512]{2,1,0:T(8,128)(2,1)} %bitcast.141, f32[512,2]{0,1:T(2,128)S(1)} %add_rsqrt_fusion, bf16[64,2,8,512]{3,2,1,0:T(8,128)(2,1)} %bitcast.128), kind=kOutput, calls=%fused_computation.26 | convolution fusion | flops 1080033280 | bytes 7344128 | tf_op jit(solution)/shard_map/thj,hoj->tho/dot_general | solution.py:99
  274.1 2.3 copy.105
  276.4 0.7 constant_dynamic-slice_fusion
  (14 shorter events, 0.1 us)
Async XLA Ops:
  7.2 247.1 %all-reduce.2.cloned.1.call-start = ((), (), s32[]{:S(2)}) async-start(), calls=%async_computation | async-start | bytes 12582912 | tf_op jit(solution)/shard_map/psum | solution.py:90
  8.7 58.8 %collective-permute-start.2 = (bf16[512,1024]{0,1:T(8,128)(2,1)S(1)}, bf16[512,1024]{0,1:T(8,128)(2,1)}, u32[]{:S(2)}, u32[]{:S(2)}) collective-permute-start(bf16[512,1024]{0,1:T(8,128)(2,1)S(1)} %copy.89), channel_id=1, source_target_pairs={{0,2},{1,3},{2,4},{3,5},{4,6},{5,7},{6,8},{7,9},{8,10},{9,11},{10,... | collective-permute-start | bytes 3145736 | tf_op jit(solution)/shard_map/ppermute | solution.py:15
  14.6 52.9 %collective-permute-start.3 = (bf16[512,1024]{0,1:T(8,128)(2,1)S(1)}, bf16[512,1024]{0,1:T(8,128)(2,1)}, u32[]{:S(2)}, u32[]{:S(2)}) collective-permute-start(bf16[512,1024]{0,1:T(8,128)(2,1)S(1)} %copy.89), channel_id=1, source_target_pairs={{0,1},{1,2},{2,3},{3,4},{4,5},{5,6},{6,7},{7,8},{8,9},{9,10},{10,1... | collective-permute-start | bytes 3145736 | tf_op jit(solution)/shard_map/ppermute | solution.py:15
  17.0 42.7 %collective-permute-start = (bf16[512,1024]{1,0:T(8,128)(2,1)}, bf16[512,1024]{1,0:T(8,128)(2,1)}, u32[]{:S(2)}, u32[]{:S(2)}) collective-permute-start(bf16[512,1024]{1,0:T(8,128)(2,1)} %param.9), channel_id=1, source_target_pairs={{0,2},{1,3},{2,4},{3,5},{4,6},{5,7},{6,8},{7,9},{8,10},{9,11},{10,... | collective-permute-start | bytes 3145736 | tf_op jit(solution)/shard_map/ppermute | solution.py:15
  20.0 39.8 %collective-permute-start.1 = (bf16[512,1024]{1,0:T(8,128)(2,1)}, bf16[512,1024]{1,0:T(8,128)(2,1)}, u32[]{:S(2)}, u32[]{:S(2)}) collective-permute-start(bf16[512,1024]{1,0:T(8,128)(2,1)} %param.9), channel_id=1, source_target_pairs={{0,1},{1,2},{2,3},{3,4},{4,5},{5,6},{6,7},{7,8},{8,9},{9,10},{10,1... | collective-permute-start | bytes 3145736 | tf_op jit(solution)/shard_map/ppermute | solution.py:15
  24.5 3.6 %copy-start.8 = (bf16[1024,512]{1,0:T(8,128)(2,1)S(1)}, bf16[1024,512]{1,0:T(8,128)(2,1)}, u32[]{:S(2)}) copy-start(bf16[1024,512]{1,0:T(8,128)(2,1)} %param.11) | copy-start | bytes 3145732
  26.1 4.1 %copy-start.5 = (bf16[1024,512]{1,0:T(8,128)(2,1)S(1)}, bf16[1024,512]{1,0:T(8,128)(2,1)}, u32[]{:S(2)}) copy-start(bf16[1024,512]{1,0:T(8,128)(2,1)} %param.12) | copy-start | bytes 3145732
  30.2 2.1 copy-start.16
  30.2 29.5 %copy-start.14 = (bf16[512,1024]{1,0:T(8,128)(2,1)S(1)}, bf16[512,1024]{1,0:T(8,128)(2,1)}, u32[]{:S(2)}) copy-start(bf16[512,1024]{1,0:T(8,128)(2,1)} %param.9) | copy-start | bytes 3145732
  67.5 1.9 copy-start.1
  69.4 2.4 copy-start.15
  71.9 2.6 copy-start.10
  74.5 7.8 %copy-start.3 = (bf16[1024,512]{1,0:T(8,128)(2,1)S(1)}, bf16[1024,512]{1,0:T(8,128)(2,1)}, u32[]{:S(2)}) copy-start(bf16[1024,512]{1,0:T(8,128)(2,1)} %param.13) | copy-start | bytes 3145732
  82.3 2.1 copy-start.11
  84.4 1.6 copy-start.12
  86.0 1.2 copy-start.13
  91.6 162.7 %copy-start.6 = (bf16[1024,512]{1,0:T(8,128)(2,1)S(1)}, bf16[1024,512]{1,0:T(8,128)(2,1)}, u32[]{:S(2)}) copy-start(bf16[1024,512]{1,0:T(8,128)(2,1)} %param.12) | copy-start | bytes 3145732
  254.3 4.9 %copy-start = (f32[3072,512]{1,0:T(8,128)S(1)}, f32[3072,512]{1,0:T(8,128)}, u32[]{:S(2)}) copy-start(f32[3072,512]{1,0:T(8,128)} %all-reduce.2.cloned.1.call-done) | copy-start | bytes 18874372
  254.3 5.2 %copy-start.4 = (bf16[1024,512]{1,0:T(8,128)(2,1)S(1)}, bf16[1024,512]{1,0:T(8,128)(2,1)}, u32[]{:S(2)}) copy-start(bf16[1024,512]{1,0:T(8,128)(2,1)} %param.13) | copy-start | bytes 3145732
  254.3 5.5 %copy-start.7 = (bf16[1024,512]{1,0:T(8,128)(2,1)S(1)}, bf16[1024,512]{1,0:T(8,128)(2,1)}, u32[]{:S(2)}) copy-start(bf16[1024,512]{1,0:T(8,128)(2,1)} %param.12) | copy-start | bytes 3145732
  254.3 5.8 %copy-start.9 = (bf16[1024,512]{1,0:T(8,128)(2,1)S(1)}, bf16[1024,512]{1,0:T(8,128)(2,1)}, u32[]{:S(2)}) copy-start(bf16[1024,512]{1,0:T(8,128)(2,1)} %param.11) | copy-start | bytes 3145732
  265.1 1.5 copy-start.2
Sparse Core Ops, SparseCore 0:
  91.7 162.5 all-reduce.1
where the time goes:
time: 284 us
  waiting for transfers between devices  188 us (66%)
  matrix products  26.9 us (9%)
  other arithmetic  24.4 us (9%)
  starting transfers between devices  15.5 us (5%)
  local copies, waits for them, and re-layouts  14.9 us (5%)
  between operations  14.2 us (5%)
    psum x1, waiting for transfers between devices, local(): summed = lax.psum(grads, 'ctx')  162 us
    ppermute x4, waiting for transfers between devices, passed_along(): lax.ppermute(value, axis, [(source, source + steps) for source in range(l...  25.5 us
    ppermute x4, starting transfers between devices, passed_along(): lax.ppermute(value, axis, [(source, source + steps) for source in range(l...  15.5 us
    dot_general x1, matrix products, local(): jnp.einsum('hqk,khd->qhd', weights, v_block, preferred_element_type=jnp.f...  7.75 us
    unnamed x36, local copies, waits for them, and re-layouts  6.35 us
  transfers between devices with their start and end apart: 5, of which 2 were waited for; matrix products, arithmetic and copies ran while one was open for 6% of the time, Pallas kernels for 0%

commit v1 on v0

--- a/solution.py
+++ b/solution.py
@@ -1,3 +1,4 @@
+import functools
 import math
 import jax
 import jax.numpy as jnp
@@ -7,6 +8,19 @@
 H = 2
 HD = 512
 WINDOW = 1024
+
+
+def _form_samples(xin, axis_tag):
+    fan = lax.axis_size(axis_tag)
+    row_out, x_next = (xin, 0)
+    while 1 << x_next < fan:
+        outcome_arr = lax.ppermute(row_out, axis_tag, [(q, q ^ 1 << x_next) for q in range(fan)])
+        row_out = row_out + outcome_arr
+        x_next = x_next + 1
+    return row_out
+
+
+remake_signs_now = functools.partial(_form_samples, axis_tag="ctx")
 
 
 def passed_along(value, axis, steps):
@@ -87,7 +101,7 @@
     old_rows = jnp.concatenate([w_gate, w_up, w_down], 0)
     own_count = grads.shape[0] // lax.axis_size("ctx")
     own_first = lax.axis_index("ctx") * own_count
-    summed = lax.psum(grads, "ctx")
+    summed = remake_signs_now(grads)
     fresh = normalize_rows(old_rows, summed)
     own_weights = lax.dynamic_slice_in_dim(fresh, own_first, own_count, 0)
     new_gate = fresh[: H * HD].reshape(H, HD, HD)

time: 284 us -> 699 us (2.46)
  waiting for transfers between devices: 188 us -> 575 us
  starting transfers between devices: 15.5 us -> 45.3 us
  between operations: 14.2 us -> 0.9 us
  other arithmetic: 24.4 us -> 36.2 us
    ppermute x0 -> x4, waiting for transfers between devices: none -> 550 us  [_form_samples(): lax.ppermute(row_out, axis_tag, [(q, q ^ 1 << x_next) for q in range(fan)])]
    psum x1 -> x0, waiting for transfers between devices: 162 us -> none  [local(): summed = lax.psum(grads, 'ctx')]
    ppermute x0 -> x4, starting transfers between devices: none -> 29.8 us  [_form_samples(): lax.ppermute(row_out, axis_tag, [(q, q ^ 1 << x_next) for q in range(fan)])]
    add x0 -> x3, other arithmetic: none -> 10.2 us  [_form_samples(): row_out = row_out + outcome_arr]
  transfers between devices with their start and end apart: 5 -> 8, of which waited for: 2 -> 5; matrix products, arithmetic and copies ran while one was open for 6% -> 3% of each run, Pallas kernels for 0% -> 0%
where the time goes in v1:
time: 699 us; the launch traced here: 698 us
  waiting for transfers between devices  575 us (82%)
  starting transfers between devices  45.3 us (6%)
  other arithmetic  36.2 us (5%)
  matrix products  26.9 us (4%)
  local copies, waits for them, and re-layouts  13.7 us (2%)
    ppermute x4, waiting for transfers between devices, _form_samples(): lax.ppermute(row_out, axis_tag, [(q, q ^ 1 << x_next) for q in range(fan)])  550 us
    ppermute x4, starting transfers between devices, _form_samples(): lax.ppermute(row_out, axis_tag, [(q, q ^ 1 << x_next) for q in range(fan)])  29.8 us
    ppermute x4, waiting for transfers between devices, passed_along(): lax.ppermute(value, axis, [(source, source + steps) for source in range(l...  25.5 us
    ppermute x4, starting transfers between devices, passed_along(): lax.ppermute(value, axis, [(source, source + steps) for source in range(l...  15.5 us
  transfers between devices with their start and end apart: 8, of which 5 were waited for; matrix products, arithmetic and copies ran while one was open for 3% of the time, Pallas kernels for 0%

profile of v1, /device:TPU:0, one launch (start us, length us, event | category | flops | bytes accessed | tf_op | source)
XLA Modules:
  0.0 698.3 jit_solution(16202132383406210350)
XLA Ops:
  0.6 1.5 copy.89
  2.1 5.9 collective-permute-start.2
  8.0 2.4 collective-permute-start.3
  10.4 2.9 collective-permute-start
  13.4 4.2 collective-permute-start.1
  17.6 0.2 multiply_reduce_fusion.1
  17.9 1.7 copy.99
  19.5 0.0 copy-start.4
  19.6 1.9 multiply_convert_fusion.1
  21.4 0.0 copy-start.8
  21.5 0.0 copy-done.6
  21.5 2.2 fusion.60
  23.7 0.0 copy-done.4
  23.7 2.1 fusion.59
  25.7 0.0 copy-done.8
  25.7 0.0 copy-done.16
  25.8 1.9 fusion.7
  27.7 25.4 %collective-permute-done = bf16[512,1024]{1,0:T(8,128)(2,1)} collective-permute-done((bf16[512,1024]{1,0:T(8,128)(2,1)}, bf16[512,1024]{1,0:T(8,128)(2,1)}, u32[]{:S(2)}, u32[]{:S(2)}) %collective-permute-start) | collective-permute-done | bytes 1048608 | tf_op jit(solution)/shard_map/ppermute | solution.py:29
  53.1 0.0 collective-permute-done.1
  53.1 0.0 copy-done.14
  53.1 3.1 pad_maximum_fusion.1
  56.2 4.7 copy.88
  60.9 0.0 collective-permute-done.2
  60.9 0.0 collective-permute-done.3
  60.9 1.9 pad_maximum_fusion.2
  62.9 0.0 copy-done.2
  62.9 0.0 copy-start.15
  62.9 2.4 fusion.31
  65.3 0.0 copy-done.15
  65.3 0.0 copy-start.10
  65.3 2.2 fusion.58
  67.5 0.4 copy-done.10
  68.0 7.7 %fusion.26 = bf16[2,512,512]{2,1,0:T(8,128)(2,1)} fusion(bf16[1536,2,512]{0,2,1:T(8,128)(2,1)} %bitcast.142, f32[2,512]{1,0:T(2,128)S(1)} %fusion.58, f32[2,1536,512]{2,1,0:T(8,128)} %copy-done.10, pred[512,1536]{0,1:T(8,128)(4,1)} %fusion.7), kind=kOutput, calls=%fused_computation.53 | convolution fusion | flops 1619003904 | bytes 11276288 | tf_op jit(solution)/shard_map/hqk,khd->qhd/dot_general | solution.py:78
  75.7 2.1 fusion.36
  77.9 0.1 copy-done.11
  77.9 0.9 fusion.27
  78.9 0.7 copy-done.12
  79.5 1.1 fusion.33
  80.6 0.1 copy-done.13
  80.8 0.9 fusion.29
  81.7 0.7 pad_maximum_fusion
  82.4 21.5 %collective-permute-start.4 = (f32[3072,512]{1,0:T(8,128)S(1)}, f32[3072,512]{1,0:T(8,128)S(1)}, u32[]{:S(2)}, u32[]{:S(2)}) collective-permute-start(f32[3072,512]{1,0:T(8,128)S(1)} %pad_maximum_fusion), channel_id=1, source_target_pairs={{0,1},{1,0},{2,3},{3,2},{4,5},{5,4},{6,7},{7,6},{8,9},{9,8},{10,11... | collective-permute-start | bytes 18874376 | tf_op jit(solution)/shard_map/ppermute | solution.py:17
  103.9 9.8 %collective-permute-done.4 = f32[3072,512]{1,0:T(8,128)S(1)} collective-permute-done((f32[3072,512]{1,0:T(8,128)S(1)}, f32[3072,512]{1,0:T(8,128)S(1)}, u32[]{:S(2)}, u32[]{:S(2)}) %collective-permute-start.4) | collective-permute-done | bytes 6291488 | tf_op jit(solution)/shard_map/ppermute | solution.py:17
  113.7 1.6 fusion.56
  115.3 2.8 collective-permute-start.5
  118.1 135.9 %collective-permute-done.5 = f32[3072,512]{1,0:T(8,128)} collective-permute-done((f32[3072,512]{1,0:T(8,128)S(1)}, f32[3072,512]{1,0:T(8,128)}, u32[]{:S(2)}, u32[]{:S(2)}) %collective-permute-start.5) | collective-permute-done | bytes 6291488 | tf_op jit(solution)/shard_map/ppermute | solution.py:17
  254.1 4.3 add.99
  258.4 2.8 collective-permute-start.6
  261.2 135.0 %collective-permute-done.6 = f32[3072,512]{1,0:T(8,128)S(1)} collective-permute-done((f32[3072,512]{1,0:T(8,128)S(1)}, f32[3072,512]{1,0:T(8,128)S(1)}, u32[]{:S(2)}, u32[]{:S(2)}) %collective-permute-start.6) | collective-permute-done | bytes 6291488 | tf_op jit(solution)/shard_map/ppermute | solution.py:17
  396.1 4.2 add.100
  400.4 2.8 collective-permute-start.7
  403.1 0.3 fusion.9
  403.4 0.0 copy-start.1
  403.4 0.0 copy-start.5
  403.4 0.0 copy-start.7
  403.4 269.1 %collective-permute-done.7 = f32[3072,512]{1,0:T(8,128)} collective-permute-done((f32[3072,512]{1,0:T(8,128)}, f32[3072,512]{1,0:T(8,128)}, u32[]{:S(2)}, u32[]{:S(2)}) %collective-permute-start.7) | collective-permute-done | bytes 6291488 | tf_op jit(solution)/shard_map/ppermute | solution.py:17
  672.5 5.8 fusion.1
  678.4 8.0 %multiply_convert_fusion = bf16[3072,512]{1,0:T(8,128)(2,1)S(1)} fusion(f32[3072]{0:T(1024)S(1)} %rsqrt_multiply_fusion, f32[3072,512]{1,0:T(8,128)} %add.100, f32[3072,512]{1,0:T(8,128)} %collective-permute-done.7, bf16[1024,512]{1,0:T(8,128)(2,1)S(1)} %copy-done.1, bf16[1024,512]{1,0:T(8,128)(2,1)S(1)} %copy-done.5, bf16[1024,512]{1,0:T(8,128)(2,1)S(1)} %copy-done.7), kind=kLoop, calls=%fused_computation.6 | loop fusion | flops 15728640 | bytes 18886656 | tf_op jit(solution)/shard_map/convert_element_type | solution.py:45
  686.4 0.0 copy-start.3
  686.4 1.5 fusion.57
  687.9 2.1 fusion.40
  690.0 5.3 fusion.11
  695.3 2.3 copy.105
  697.6 0.7 constant_dynamic-slice_fusion
  (22 shorter events, 0.1 us)
Async XLA Ops:
  2.1 58.8 %collective-permute-start.2 = (bf16[512,1024]{0,1:T(8,128)(2,1)S(1)}, bf16[512,1024]{0,1:T(8,128)(2,1)}, u32[]{:S(2)}, u32[]{:S(2)}) collective-permute-start(bf16[512,1024]{0,1:T(8,128)(2,1)S(1)} %copy.89), channel_id=1, source_target_pairs={{0,2},{1,3},{2,4},{3,5},{4,6},{5,7},{6,8},{7,9},{8,10},{9,11},{10,... | collective-permute-start | bytes 3145736 | tf_op jit(solution)/shard_map/ppermute | solution.py:29
  8.0 52.9 %collective-permute-start.3 = (bf16[512,1024]{0,1:T(8,128)(2,1)S(1)}, bf16[512,1024]{0,1:T(8,128)(2,1)}, u32[]{:S(2)}, u32[]{:S(2)}) collective-permute-start(bf16[512,1024]{0,1:T(8,128)(2,1)S(1)} %copy.89), channel_id=1, source_target_pairs={{0,1},{1,2},{2,3},{3,4},{4,5},{5,6},{6,7},{7,8},{8,9},{9,10},{10,1... | collective-permute-start | bytes 3145736 | tf_op jit(solution)/shard_map/ppermute | solution.py:29
  10.4 42.7 %collective-permute-start = (bf16[512,1024]{1,0:T(8,128)(2,1)}, bf16[512,1024]{1,0:T(8,128)(2,1)}, u32[]{:S(2)}, u32[]{:S(2)}) collective-permute-start(bf16[512,1024]{1,0:T(8,128)(2,1)} %param.9), channel_id=1, source_target_pairs={{0,2},{1,3},{2,4},{3,5},{4,6},{5,7},{6,8},{7,9},{8,10},{9,11},{10,... | collective-permute-start | bytes 3145736 | tf_op jit(solution)/shard_map/ppermute | solution.py:29
  13.4 39.8 %collective-permute-start.1 = (bf16[512,1024]{1,0:T(8,128)(2,1)}, bf16[512,1024]{1,0:T(8,128)(2,1)}, u32[]{:S(2)}, u32[]{:S(2)}) collective-permute-start(bf16[512,1024]{1,0:T(8,128)(2,1)} %param.9), channel_id=1, source_target_pairs={{0,1},{1,2},{2,3},{3,4},{4,5},{5,6},{6,7},{7,8},{8,9},{9,10},{10,1... | collective-permute-start | bytes 3145736 | tf_op jit(solution)/shard_map/ppermute | solution.py:29
  17.9 3.6 copy-start.6
  19.5 4.1 copy-start.4
  21.4 4.3 copy-start.8
  23.6 2.1 copy-start.16
  23.6 29.5 %copy-start.14 = (bf16[512,1024]{1,0:T(8,128)(2,1)S(1)}, bf16[512,1024]{1,0:T(8,128)(2,1)}, u32[]{:S(2)}) copy-start(bf16[512,1024]{1,0:T(8,128)(2,1)} %param.9) | copy-start | bytes 3145732
  60.9 1.9 copy-start.2
  62.9 2.4 copy-start.15
  65.3 2.7 copy-start.10
  68.0 7.8 %copy-start = (bf16[1024,512]{1,0:T(8,128)(2,1)S(1)}, bf16[1024,512]{1,0:T(8,128)(2,1)}, u32[]{:S(2)}) copy-start(bf16[1024,512]{1,0:T(8,128)(2,1)} %param.13) | copy-start | bytes 3145732
  75.7 2.1 copy-start.9
  75.7 2.2 copy-start.11
  77.9 1.6 copy-start.12
  79.5 1.2 copy-start.13
  82.4 31.3 %collective-permute-start.4 = (f32[3072,512]{1,0:T(8,128)S(1)}, f32[3072,512]{1,0:T(8,128)S(1)}, u32[]{:S(2)}, u32[]{:S(2)}) collective-permute-start(f32[3072,512]{1,0:T(8,128)S(1)} %pad_maximum_fusion), channel_id=1, source_target_pairs={{0,1},{1,0},{2,3},{3,2},{4,5},{5,4},{6,7},{7,6},{8,9},{9,8},{10,11... | collective-permute-start | bytes 18874376 | tf_op jit(solution)/shard_map/ppermute | solution.py:17
  115.3 138.7 %collective-permute-start.5 = (f32[3072,512]{1,0:T(8,128)S(1)}, f32[3072,512]{1,0:T(8,128)}, u32[]{:S(2)}, u32[]{:S(2)}) collective-permute-start(f32[3072,512]{1,0:T(8,128)S(1)} %fusion.56), channel_id=1, source_target_pairs={{0,2},{1,3},{2,0},{3,1},{4,6},{5,7},{6,4},{7,5},{8,10},{9,11},{10,... | collective-permute-start | bytes 18874376 | tf_op jit(solution)/shard_map/ppermute | solution.py:17
  258.4 137.7 %collective-permute-start.6 = (f32[3072,512]{1,0:T(8,128)S(1)}, f32[3072,512]{1,0:T(8,128)S(1)}, u32[]{:S(2)}, u32[]{:S(2)}) collective-permute-start(f32[3072,512]{1,0:T(8,128)S(1)} %add.99), channel_id=1, source_target_pairs={{0,4},{1,5},{2,6},{3,7},{4,0},{5,1},{6,2},{7,3},{8,12},{9,13},{10,... | collective-permute-start | bytes 18874376 | tf_op jit(solution)/shard_map/ppermute | solution.py:17
  400.4 272.1 %collective-permute-start.7 = (f32[3072,512]{1,0:T(8,128)}, f32[3072,512]{1,0:T(8,128)}, u32[]{:S(2)}, u32[]{:S(2)}) collective-permute-start(f32[3072,512]{1,0:T(8,128)} %add.100), channel_id=1, source_target_pairs={{0,8},{1,9},{2,10},{3,11},{4,12},{5,13},{6,14},{7,15},{8,0},{9,1},... | collective-permute-start | bytes 18874376 | tf_op jit(solution)/shard_map/ppermute | solution.py:17
  403.4 275.0 %copy-start.1 = (bf16[1024,512]{1,0:T(8,128)(2,1)S(1)}, bf16[1024,512]{1,0:T(8,128)(2,1)}, u32[]{:S(2)}) copy-start(bf16[1024,512]{1,0:T(8,128)(2,1)} %param.13) | copy-start | bytes 3145732
  403.4 275.0 %copy-start.5 = (bf16[1024,512]{1,0:T(8,128)(2,1)S(1)}, bf16[1024,512]{1,0:T(8,128)(2,1)}, u32[]{:S(2)}) copy-start(bf16[1024,512]{1,0:T(8,128)(2,1)} %param.12) | copy-start | bytes 3145732
  403.4 275.0 %copy-start.7 = (bf16[1024,512]{1,0:T(8,128)(2,1)S(1)}, bf16[1024,512]{1,0:T(8,128)(2,1)}, u32[]{:S(2)}) copy-start(bf16[1024,512]{1,0:T(8,128)(2,1)} %param.11) | copy-start | bytes 3145732
  686.4 1.5 copy-start.3
